TPU v7x, 32 devices: a whole 2x2x4 slice. The times are simulated.
32 devices in a mesh: group: 2 (over y), tm: 16 (over z, x, core), height: 1.
Axes of the slice: x: 2, y: 2, z: 4, core: 2. Of those that a mesh axis runs over, the one named last changes fastest.
Arguments:
- query: bfloat16 [32, 2, 64, 1536], P(('group', 'tm'), 'height'), parts along dimension 0
- cur_kv: bfloat16 [2, 32, 2, 64, 1536], P(None, ('group', 'tm'), 'height'), parts along dimension 1
- cur_pos: int32 [3, 32, 2, 64], P(None, ('group', 'tm'), 'height'), parts along dimension 1, may hold values from 0 to 63
- cache_kv: bfloat16 [32, 2, 32, 1536], P(('group', 'tm'), None, 'height'), parts along dimension 0
- cache_pos: int32 [32, 3, 32], P(('group', 'tm'), None, 'height'), parts along dimension 0, may hold values from 0 to 63
- counts: int32 [32, 1], P(('group', 'tm'), 'height'), parts along dimension 0, may hold values from 1 to 32
- visible: int32 [32, 16], P(('group', 'tm')), parts along dimension 0, may hold values 0 or 1
Outputs:
- attended: bfloat16 [32, 2, 64, 1536], P(('group', 'tm'), 'height'), parts along dimension 0
There are 2 independent parts, one for each index of `group`. A program takes and returns all parts, laid end to end along the dimension named above; each array names one. Nothing has to cross between parts.
Inputs may be any that keep to these rules, and one draw needn't show every extreme that they name: `counts`: every earlier span has at least one live slot in each row tile.
All inputs are finite; a program needn't handle non-finite values. No bound on the sum of `visible` on one device may be relied on, other than what follows from the above.
Results may differ from a plain program's by a relative error of at most 0.006.
The roundings to bfloat16 on the way count: a program that leaves them out, or rounds other values in their place, can miss the bound.
Values may be sent and summed in bfloat16 or wider, within the bound.
A program may use at most 64 MiB of HBM per device.

v0:
```python
import jax
import jax.numpy as jnp
from jax import lax
from jax.sharding import PartitionSpec as P

HEADS = 12
HEAD = 128
REACH = 2


masked_value = -1e30


def extended(cells, sides, width):
    for axis, dim in sides:
        count = lax.axis_size(axis)
        ends = count - 1
        head = lax.slice_in_dim(cells, 0, width, axis=dim)
        tail = lax.slice_in_dim(cells, cells.shape[dim] - width, cells.shape[dim], axis=dim)
        cells = jnp.concatenate(
            [
                lax.ppermute(tail, axis, [(i, (i + 1) % count) for i in range(ends)]),
                cells,
                lax.ppermute(head, axis, [((i + 1) % count, i) for i in range(ends)]),
            ],
            axis=dim,
        )
    return cells


def rope_tables():
    half = HEAD // 2
    index = jnp.arange(half)
    first = HEAD // 8
    second = 3 * HEAD // 16
    member = (index >= first).astype(jnp.int32) + (index >= first + second).astype(jnp.int32)
    begin = jnp.where(member == 0, 0, jnp.where(member == 1, first, first + second))
    length = jnp.where(member == 0, first, jnp.where(member == 1, second, half - first - second))
    frequency = jnp.power(
        10000.0, -(index - begin).astype(jnp.float32) / length.astype(jnp.float32)
    )
    select = (member[None, :] == jnp.arange(3)[:, None]).astype(jnp.float32) * frequency[None, :]
    return select


def rotate(vectors, pos_time, pos_row, pos_column):
    select = rope_tables()
    angle = (
        pos_time.astype(jnp.float32)[..., None] * select[0]
        + pos_row.astype(jnp.float32)[..., None] * select[1]
        + pos_column.astype(jnp.float32)[..., None] * select[2]
    )
    cosine = jnp.cos(angle)[..., None, :]
    sine = jnp.sin(angle)[..., None, :]
    shaped = vectors.astype(jnp.float32).reshape(vectors.shape[:-1] + (HEADS, 2, HEAD // 2))
    lower = shaped[..., 0, :]
    upper = shaped[..., 1, :]
    turned = jnp.stack([lower * cosine - upper * sine, upper * cosine + lower * sine], axis=-2)
    return turned.reshape(vectors.shape).astype(jnp.bfloat16)


def per_device(query, cur_kv, cur_pos, cache_kv, cache_pos, counts, visible):
    frames, tile_rows, columns, depth = query.shape
    queries = tile_rows * columns
    scale = HEAD ** (-0.5)
    tile_index = lax.axis_index("height")
    frame_rows = tile_rows * lax.axis_size("height")
    q_rot = rotate(query, cur_pos[0], cur_pos[1], cur_pos[2]).reshape(frames, queries, HEADS, HEAD)
    q_heads = jnp.transpose(q_rot, (0, 2, 1, 3))
    k_rot = rotate(cur_kv[0], cur_pos[0], cur_pos[1], cur_pos[2])
    local_pair = jnp.stack([k_rot, cur_kv[1]])
    padded = extended(local_pair, (("height", 2),), REACH)
    extent = tile_rows + 2 * REACH
    local_keys = jnp.transpose(
        padded[0].reshape(frames, extent * columns, HEADS, HEAD), (0, 2, 1, 3)
    )
    local_values = jnp.transpose(
        padded[1].reshape(frames, extent * columns, HEADS, HEAD), (0, 2, 1, 3)
    )
    query_row = tile_index * tile_rows + jnp.arange(queries) // columns
    key_row = tile_index * tile_rows - REACH + jnp.arange(extent * columns) // columns
    local_ok = (
        (key_row[None, :] >= 0)
        & (key_row[None, :] < frame_rows)
        & (jnp.abs(query_row[:, None] - key_row[None, :]) <= REACH)
    )
    local_bias = jnp.where(local_ok, 0.0, masked_value).astype(jnp.float32)
    scores = (
        jnp.einsum("fhqd,fhkd->fhqk", q_heads, local_keys, preferred_element_type=jnp.float32)
        * scale
        + local_bias[None, None]
    )
    highest = jnp.max(scores, axis=-1)
    weights = jnp.exp(scores - highest[..., None])
    totals = jnp.sum(weights, axis=-1)
    summed = jnp.einsum(
        "fhqk,fhkd->fhqd",
        weights.astype(jnp.bfloat16),
        local_values,
        preferred_element_type=jnp.float32,
    )
    slots = cache_kv.shape[2]
    slot_index = jnp.arange(slots)
    pair_piece = lax.all_gather(cache_kv, "tm", axis=0, tiled=True)
    position_piece = lax.all_gather(cache_pos, "tm", axis=0, tiled=True)
    count_piece = lax.all_gather(counts, "tm", axis=0, tiled=True)
    turned = rotate(
        pair_piece[:, 0], position_piece[:, 0], position_piece[:, 1], position_piece[:, 2]
    )
    blocks = turned.shape[0]
    live = count_piece[:, 0]
    usable = (
        (visible[:, :, None] > 0) & (slot_index[None, None, :] < live[None, :, None])
    ).reshape(frames, blocks * slots)
    block_bias = jnp.where(usable, 0.0, masked_value).astype(jnp.float32)
    flat_keys = jnp.transpose(turned.reshape(blocks * slots, HEADS, HEAD), (1, 0, 2))
    flat_values = jnp.transpose(pair_piece[:, 1].reshape(blocks * slots, HEADS, HEAD), (1, 0, 2))
    block_scores = (
        jnp.einsum("fhqd,hkd->fhqk", q_heads, flat_keys, preferred_element_type=jnp.float32) * scale
        + block_bias[:, None, None, :]
    )
    new_max = jnp.maximum(highest, jnp.max(block_scores, axis=-1))
    block_weights = jnp.exp(block_scores - new_max[..., None])
    fading = jnp.exp(highest - new_max)
    added = jnp.einsum(
        "fhqk,hkd->fhqd",
        block_weights.astype(jnp.bfloat16),
        flat_values,
        preferred_element_type=jnp.float32,
    )
    final_total = totals * fading + jnp.sum(block_weights, axis=-1)
    final_sum = summed * fading[..., None] + added
    output = (final_sum / final_total[..., None]).astype(jnp.bfloat16)
    output = jnp.transpose(output, (0, 2, 1, 3))
    return output.reshape(frames, tile_rows, columns, depth)


def solution(mesh):
    in_specs = (
        P(("group", "tm"), "height", None, None),
        P(None, ("group", "tm"), "height", None, None),
        P(None, ("group", "tm"), "height", None),
        P(("group", "tm"), None, "height", None),
        P(("group", "tm"), None, "height"),
        P(("group", "tm"), "height"),
        P(("group", "tm"), None),
    )
    out_specs = P(("group", "tm"), "height", None, None)
    return jax.shard_map(
        per_device, mesh=mesh, in_specs=in_specs, out_specs=out_specs, check_vma=False
    )
```

profile of v0, /device:TPU:1, one launch (start us, length us, event | category | flops | bytes accessed | tf_op | source)
XLA Modules:
  0.0 136.4 jit_solution(14156414083360277095)
XLA Ops:
  9.6 2.3 %reshape.430 = f32[1,2,64,12,2,64]{5,4,3,2,1,0:T(2,128)S(1)} reshape(bf16[1,2,64,1536]{3,2,1,0:T(8,128)(2,1)} %param.7) | data formatting | bytes 1179648 | tf_op jit(solution)/shard_map/reshape | solution.py:55
  13.1 2.5 %fusion.74 = (f32[1,2,64,12,1,64]{5,4,3,2,1,0:T(1,128)S(1)}, f32[1,2,64,12,1,64]{5,4,3,2,1,0:T(1,128)S(1)}, f32[1,2,64,12,1,64]{5,4,3,2,1,0:T(1,128)S(1)}, f32[1,2,64,12,1,64]{5,4,3,2,1,0:T(1,128)S(1)}) fusion(f32[1,2,64,12,2,64]{5,4,3,2,1,0:T(2,128)S(1)} %reshape.430, f32[1,2,64,12,2,64]{5,4,3,2,1,0:T(2,128)S(1)} %reshape.431), kind=kLoop, calls=%fused_computation.104 | loop fusion | bytes 3145728 | tf_op jit(solution)/shard_map/slice | solution.py:56
  15.5 3.4 %subtract_convert_fusion.2 = (bf16[1,2,64,12,1,64]{5,4,2,1,3,0:T(2,128)(2,1)S(1)}, bf16[1,2,64,12,1,64]{5,4,2,1,3,0:T(2,128)(2,1)S(1)}, bf16[1,2,64,12,1,64]{5,4...) fusion(f32[1,2,64,12,1,64]{5,4,3,2,1,0:T(1,128)S(1)} %get-tuple-element.20, ...), kind=kLoop, calls=%fused_computation.46 | loop fusion | flops 1572864 | bytes 2424832 | tf_op jit(solution)/shard_map/convert.7
  19.0 2.1 %pad_maximum_fusion.3 = bf16[1,2,64,12,2,64]{5,4,2,1,3,0:T(2,128)(2,1)S(1)} fusion(bf16[1,2,64,12,1,64]{5,4,2,1,3,0:T(2,128)(2,1)S(1)} %get-tuple-element.25, bf16[1,2,64,12,1,64]{5,4,2,1,3,0:T(2,128)(2,1)S(1)} %get-tuple-element.26), kind=kLoop, calls=%fused_computation.41 | loop fusion | flops 786432 | bytes 786432 | tf_op jit(solution)/shard_map/stack | solution.py:58
  24.4 1.7 %collective-permute-start = (bf16[2,1,2,64,1536]{4,3,2,1,0:T(8,128)(2,1)}, bf16[2,1,2,64,1536]{4,3,2,1,0:T(8,128)(2,1)}, u32[]{:S(2)}, u32[]{:S(2)}) collective-permute-start(bf16[2,1,2,64,1536]{4,3,2,1,0:T(8,128)(2,1)} %pad_maximum_fusion.4), channel_id=1, source_target_pairs={} | collective-permute-start | bytes 2359304 | tf_op jit(solution)/shard_map/ppermute | solution.py:22
  26.0 11.6 %all-reduce = s32[16]{0:T(128)} all-reduce(s32[16]{0:T(128)S(1)} %bitcast_dynamic-update-slice_fusion), channel_id=1, replica_groups=mesh['group'=2,'tm'=16,'height'=1] {'tm'}, use_global_device_ids=true, to_apply=%add | all-reduce | flops 16 | bytes 128
  37.7 2.1 %pad_maximum_fusion.2 = bf16[1,2,64,12,2,64]{5,4,2,1,3,0:T(2,128)(2,1)S(1)} fusion(bf16[1,2,64,12,1,64]{5,4,2,1,3,0:T(2,128)(2,1)S(1)} %get-tuple-element.16, bf16[1,2,64,12,1,64]{5,4,2,1,3,0:T(2,128)(2,1)S(1)} %get-tuple-element.15), kind=kLoop, calls=%fused_computation.40 | loop fusion | flops 786432 | bytes 786432 | tf_op jit(solution)/shard_map/stack | solution.py:58
  41.9 20.5 %all_gather.12 = s32[16,3,32]{2,1,0:T(4,128)S(1)} all-gather(s32[1,3,32]{2,1,0:T(4,128)S(1)} %copy.36), channel_id=1, replica_groups=mesh['group'=2,'tm'=16,'height'=1] {'tm'}, dimensions={0}, use_global_device_ids=true | all-gather | bytes 6528 | tf_op jit(solution)/shard_map/all_gather | solution.py:105
  63.2 1.9 %fusion.54 = (f32[16,32,64]{2,1,0:T(8,128)}, f32[16,32,64]{2,1,0:T(8,128)}) fusion(f32[64]{0:T(128)S(1)} %get-tuple-element.38, f32[16,32]{1,0:T(8,128)S(1)} %bitcast.156, f32[64]{0:T(128)S(1)} %get-tuple-element.39, f32[16,32]{1,0:T(8,128)S(1)} %bitcast.157, f32[64]{0:T(128)S(1)} %get-tuple-element.37, f32[16,32]{1,0:T(8,128)S(1)} %bitcast.155), kind=kLoop, calls=%fused_computation.52 | loop fusion | flops 163840 | bytes 269056 | tf_op jit(solution)/shard_map/cos | solution.py:53
  65.0 1.6 %pad_maximum_fusion.1 = bf16[2,1,6,64,1536]{4,3,2,1,0:T(8,128)(2,1)S(1)} fusion(bf16[2,1,2,64,1536]{4,3,2,1,0:T(8,128)(2,1)} %collective-permute-done, bf16[1,1,2,64,1536]{4,3,2,1,0:T(8,128)(2,1)S(1)} %copy-done.3, bf16[1,1,2,64,1536]{4,3,2,1,0:T(8,128)(2,1)S(1)} %convert_element_type.231), kind=kLoop, calls=%fused_computation.9 | loop fusion | flops 3538944 | bytes 3932160 | tf_op jit(solution)/shard_map/concatenate | solution.py:20
  66.7 1.2 fusion.73
  67.9 2.5 %reshape_squeeze.9 = bf16[1,384,12,128]{3,2,1,0:T(8,128)(2,1)S(1)} reshape(bf16[1,1,6,64,1536]{4,3,2,1,0:T(8,128)(2,1)} %get-tuple-element.14) | data formatting | bytes 2359296 | tf_op jit(solution)/shard_map/reshape;squeeze | solution.py:75
  70.4 1.8 %reshape_squeeze.10 = bf16[1,384,12,128]{3,2,1,0:T(8,128)(2,1)} reshape(bf16[1,1,6,64,1536]{4,3,2,1,0:T(8,128)(2,1)S(1)} %get-tuple-element.13) | data formatting | bytes 2359296 | tf_op jit(solution)/shard_map/reshape;squeeze | solution.py:78
  73.2 1.4 %copy-done = f32[12,128,384]{2,1,0:T(8,128)} copy-done((f32[12,128,384]{2,1,0:T(8,128)}, f32[12,128,384]{2,1,0:T(8,128)S(1)}, u32[]{:S(2)}) %copy-start) | copy-done | bytes 2359320
  75.4 3.5 %fusion.72 = (bf16[16,1,32,1536]{3,2,1,0:T(8,128)(2,1)}, f32[16,1,32,1536]{3,2,1,0:T(8,128)S(1)}) fusion(bf16[16,2,32,1536]{3,2,1,0:T(8,128)(2,1)} %all-gather.2.cloned.1.call-done), kind=kLoop, calls=%fused_computation.102 | loop fusion | flops 786432 | bytes 7864320 | tf_op jit(solution)/shard_map/slice | solution.py:117
  78.9 5.7 %reshape.432 = f32[16,32,12,2,64]{4,3,2,1,0:T(2,128)} reshape(f32[16,1,32,1536]{3,2,1,0:T(8,128)S(1)} %get-tuple-element.12) | data formatting | bytes 6291456 | tf_op jit(solution)/shard_map/convert_element_type | solution.py:55
  84.7 12.7 %fusion.71 = (f32[16,32,12,1,64]{4,3,2,1,0:T(1,128)S(1)}, f32[16,32,12,1,64]{4,3,2,1,0:T(1,128)}) fusion(f32[16,32,12,2,64]{4,3,2,1,0:T(2,128)} %reshape.432), kind=kLoop, calls=%fused_computation.101 | loop fusion | bytes 6291456 | tf_op jit(solution)/shard_map/slice | solution.py:56
  97.4 7.8 %subtract_convert_fusion = (bf16[16,32,12,1,64]{4,3,1,0,2:T(2,128)(2,1)S(1)}, bf16[16,32,12,1,64]{4,3,1,0,2:T(2,128)(2,1)S(1)}) fusion(f32[16,32,12,1,64]{4,3,2,1,0:T(1,128)} %get-tuple-element.10, f32[16,32,12,1,64]{4,3,2,1,0:T(1,128)S(1)} %get-tuple-element.9, f32[16,32,64]{2,1,0:T(8,128)} %get-tuple-element.31, f32[16,32,64]{2,1,0:T(8,128)} %get-tuple-element.30), kind=kLoop, calls=%fused_computation.6 | loop fusion | flops 3145728 | bytes 4980736 | tf_op jit(solution)/shard_map/convert.3
  105.2 8.4 %pad_maximum_fusion = bf16[16,32,12,2,64]{4,3,1,0,2:T(2,128)(2,1)S(1)} fusion(bf16[16,32,12,1,64]{4,3,1,0,2:T(2,128)(2,1)S(1)} %get-tuple-element.8, bf16[16,32,12,1,64]{4,3,1,0,2:T(2,128)(2,1)S(1)} %get-tuple-element.7), kind=kLoop, calls=%fused_computation | loop fusion | flops 3145728 | bytes 3145728 | tf_op jit(solution)/shard_map/stack | solution.py:58
  113.5 2.6 %convert_element_type.241 = bf16[512,12,128]{2,0,1:T(8,128)(2,1)} reshape(bf16[16,32,12,2,64]{4,3,1,0,2:T(2,128)(2,1)S(1)} %pad_maximum_fusion) | data formatting | bytes 3145728 | tf_op jit(solution)/shard_map/convert_element_type | solution.py:59
  116.1 2.0 %bitcast_reduce_fusion = (f32[12,128]{1,0:T(8,128)S(1)}, f32[12,512,128]{2,1,0:T(8,128)S(1)}) fusion(f32[512]{0:T(512)} %and_select_fusion, bf16[1,128,12,128]{3,1,2,0:T(8,128)(2,1)S(1)} %convert_element_type.228, bf16[512,12,128]{2,0,1:T(8,128)(2,1)} %convert_element_type.241), kind=kOutput, calls=%fused_computation.2 | convolution fusion | flops 203684352 | bytes 5120000 | tf_op jit(solution)/shard_map/fhqd,hkd->fhqk/dot_general | solution.py:119
  118.2 4.0 %reshape_squeeze.11 = bf16[512,12,128]{2,1,0:T(8,128)(2,1)} reshape(bf16[16,1,32,1536]{3,2,1,0:T(8,128)(2,1)} %get-tuple-element.11) | data formatting | bytes 3145728 | tf_op jit(solution)/shard_map/reshape;squeeze | solution.py:117
  123.8 2.7 %fusion.21 = f32[1,12,128,128]{3,2,1,0:T(8,128)S(1)} fusion(f32[12,128,384]{2,1,0:T(8,128)S(1)} %copy-done.1, bf16[1,384,12,128]{3,2,1,0:T(8,128)(2,1)} %reshape_squeeze.10, f32[12,128]{1,0:T(8,128)S(1)} %get-tuple-element.40, f32[128,384]{1,0:T(8,128)S(1)} %copy-done.6, f32[12,128]{1,0:T(8,128)S(1)} %get-tuple-element.6), kind=kOutput, calls=%fused_computation.27 | convolution fusion | flops 153550848 | bytes 4534272 | tf_op jit(solution)/shard_map/fhqk,fhkd->fhqd/dot_general | solution.py:96
  126.6 1.6 %fusion.46 = bf16[1,128,12,128]{3,1,2,0:T(8,128)(2,1)S(1)} fusion(f32[1,12,128,128]{3,2,1,0:T(8,128)S(1)} %fusion.21, bf16[512,12,128]{2,1,0:T(8,128)(2,1)S(1)} %copy-done.4, f32[12,512,128]{2,1,0:T(8,128)S(1)} %get-tuple-element.43, f32[12,128]{1,0:T(8,128)S(1)} %max.17, f32[512]{0:T(512)S(1)} %copy-done.7, f32[12,128]{1,0:T(8,128)S(1)} %get-tuple-element.5), kind=kOutput, calls=%fused_computation.39 | convolution fusion | flops 205062144 | bytes 5912576 | tf_op jit(solution)/shard_map/fhqk,hkd->fhqd/dot_general | solution.py:125
  (61 shorter events, 14.2 us)
Async XLA Ops:
  6.5 68.8 %all-gather.2.cloned.1.call-start = ((), (), s32[]{:S(2)}) async-start(), calls=%async_computation | async-start | bytes 3342336 | tf_op jit(solution)/shard_map/all_gather | solution.py:104
  8.5 14.9 %copy-start.2 = (bf16[1,1,2,64,1536]{4,3,2,1,0:T(8,128)(2,1)}, bf16[1,1,2,64,1536]{4,3,2,1,0:T(8,128)(2,1)S(1)}, u32[]{:S(2)}) copy-start(bf16[1,1,2,64,1536]{4,3,2,1,0:T(8,128)(2,1)S(1)} %get-tuple-element.24) | copy-start | bytes 1179652
  8.5 4.2 %copy-start.8 = (s32[3,1,2,64]{3,2,1,0:T(2,128)S(1)}, s32[3,1,2,64]{3,2,1,0:T(2,128)}, u32[]{:S(2)}) copy-start(s32[3,1,2,64]{3,2,1,0:T(2,128)} %param.9) | copy-start | bytes 4612
  19.0 3.1 %copy-start.10 = (u32[32]{0:T(128)S(1)}, u32[32]{0:T(128)}, u32[]{:S(2)}) copy-start(u32[32]{0:T(128)} %constant.76) | copy-start | bytes 388
  23.4 16.7 %copy-start.9 = (s32[1,3,32]{2,0,1:T(1,128)S(1)}, s32[1,3,32]{2,0,1:T(1,128)}, u32[]{:S(2)}) copy-start(s32[1,3,32]{2,0,1:T(1,128)} %param.11) | copy-start | bytes 1156
  24.4 40.7 %copy-start.3 = (bf16[1,1,2,64,1536]{4,3,2,1,0:T(8,128)(2,1)S(1)}, bf16[1,1,2,64,1536]{4,3,2,1,0:T(8,128)(2,1)}, u32[]{:S(2)}) copy-start(bf16[1,1,2,64,1536]{4,3,2,1,0:T(8,128)(2,1)} %copy-done.2) | copy-start | bytes 1179652
  24.4 40.7 %collective-permute-start = (bf16[2,1,2,64,1536]{4,3,2,1,0:T(8,128)(2,1)}, bf16[2,1,2,64,1536]{4,3,2,1,0:T(8,128)(2,1)}, u32[]{:S(2)}, u32[]{:S(2)}) collective-permute-start(bf16[2,1,2,64,1536]{4,3,2,1,0:T(8,128)(2,1)} %pad_maximum_fusion.4), channel_id=1, source_target_pairs={} | collective-permute-start | bytes 2359304 | tf_op jit(solution)/shard_map/ppermute | solution.py:22
  63.2 10.0 %copy-start.5 = (f32[128,384]{1,0:T(8,128)}, f32[128,384]{1,0:T(8,128)S(1)}, u32[]{:S(2)}) copy-start(f32[128,384]{1,0:T(8,128)S(1)} %fusion.56) | copy-start | bytes 589828
  73.2 1.4 %copy-start = (f32[12,128,384]{2,1,0:T(8,128)}, f32[12,128,384]{2,1,0:T(8,128)S(1)}, u32[]{:S(2)}) copy-start(f32[12,128,384]{2,1,0:T(8,128)S(1)} %get-tuple-element.41) | copy-start | bytes 7077892
  118.1 4.0 %copy-start.7 = (f32[512]{0:T(512)S(1)}, f32[512]{0:T(512)}, u32[]{:S(2)}) copy-start(f32[512]{0:T(512)} %and_select_fusion) | copy-start | bytes 6148
  122.2 1.7 %copy-start.1 = (f32[12,128,384]{2,1,0:T(8,128)S(1)}, f32[12,128,384]{2,1,0:T(8,128)}, u32[]{:S(2)}) copy-start(f32[12,128,384]{2,1,0:T(8,128)} %copy-done) | copy-start | bytes 7077892
  122.2 1.7 %copy-start.6 = (f32[128,384]{1,0:T(8,128)S(1)}, f32[128,384]{1,0:T(8,128)}, u32[]{:S(2)}) copy-start(f32[128,384]{1,0:T(8,128)} %copy-done.5) | copy-start | bytes 589828
  123.8 2.8 %copy-start.4 = (bf16[512,12,128]{2,1,0:T(8,128)(2,1)S(1)}, bf16[512,12,128]{2,1,0:T(8,128)(2,1)}, u32[]{:S(2)}) copy-start(bf16[512,12,128]{2,1,0:T(8,128)(2,1)} %reshape_squeeze.11) | copy-start | bytes 4718596
Sparse Core Ops, SparseCore 0:
  9.6 48.0 all-gather.1
where the time goes:
time: 137 us; the launch traced here: 136 us
  local copies, waits for them, and re-layouts  44 us (32%)
  other arithmetic  36.1 us (26%)
  blocking collectives  32.2 us (24%)
  between operations  14.4 us (11%)
  matrix products  7.29 us (5%)
  starting transfers between devices  1.67 us (1%)
    all_gather x1, blocking collectives, per_device(): position_piece = lax.all_gather(cache_pos, 'tm', axis=0, tiled=True)  20.5 us
    slice x2, local copies, waits for them, and re-layouts, rotate(): lower = shaped[..., 0, :]  15.2 us
    another operation x3, other arithmetic, rotate(): jnp.stack([lower * cosine - upper * sine, upper * cosine + lower * sine],...  12.5 us
    unnamed x1, blocking collectives  11.6 us
    another operation x2, other arithmetic  11.2 us
    convert_element_type x2, local copies, waits for them, and re-layouts, rotate(): vectors.astype(jnp.float32)  6.85 us
    another operation x1, local copies, waits for them, and re-layouts, per_device(): pair_piece[:, 1].reshape(blocks * slots, HEADS, HEAD)  4.01 us
    unnamed x26, local copies, waits for them, and re-layouts  3.65 us
  transfers between devices with their start and end apart: 2, of which 0 were waited for; matrix products, arithmetic and copies ran while one was open for 23% of the time, Pallas kernels for 0%

commit v1 on v0

--- a/solution.py
+++ b/solution.py
@@ -1,6 +1,8 @@
 import jax
 import jax.numpy as jnp
 from jax import lax
+from jax.experimental import pallas as pl
+from jax.experimental.pallas import tpu as pltpu
 from jax.sharding import PartitionSpec as P
 
 HEADS = 12
@@ -135,6 +137,308 @@
     return output.reshape(frames, tile_rows, columns, depth)
 
 
+CORES = 2
+COLUMNS = 2
+LANE = CORES * COLUMNS
+DIRECTIONS = 4
+
+
+def frequency_rows(axis, shape):
+    half = HEAD // 2
+    index = lax.broadcasted_iota(jnp.int32, shape, axis) % half
+    first = HEAD // 8
+    second = 3 * HEAD // 16
+    member = (index >= first).astype(jnp.int32) + (index >= first + second).astype(jnp.int32)
+    begin = jnp.where(member == 0, 0, jnp.where(member == 1, first, first + second))
+    length = jnp.where(member == 0, first, jnp.where(member == 1, second, half - first - second))
+    ratio = (index - begin).astype(jnp.float32) / length.astype(jnp.float32)
+    return member, jnp.exp(-ratio * 9.210340371976184)
+
+
+def turn_tables(pos_time, pos_row, pos_column):
+    tokens = pos_time.shape[-1]
+    member, _ = frequency_rows(0, (HEAD, tokens))
+    chosen = jnp.where(member == 0, pos_time, jnp.where(member == 1, pos_row, pos_column))
+    eye = (
+        lax.broadcasted_iota(jnp.int32, (tokens, tokens), 0)
+        == lax.broadcasted_iota(jnp.int32, (tokens, tokens), 1)
+    ).astype(jnp.float32).astype(jnp.bfloat16)
+    spread = lax.dot_general(
+        eye,
+        chosen.astype(jnp.float32).astype(jnp.bfloat16),
+        (((1,), (1,)), ((), ())),
+        preferred_element_type=jnp.float32,
+    )
+    _, frequency = frequency_rows(1, (1, HEAD))
+    angle = spread * frequency
+    lane = lax.broadcasted_iota(jnp.int32, (tokens, HEAD), 1)
+    sine = jnp.sin(angle)
+    return jnp.cos(angle), jnp.where(lane < HEAD // 2, -sine, sine)
+
+
+def turn(vectors, cosine, sine):
+    wide = vectors.astype(jnp.float32)
+    return (wide * cosine + pltpu.roll(wide, HEAD // 2, 1) * sine).astype(jnp.bfloat16)
+
+
+def head_columns(h):
+    return slice(h * HEAD, (h + 1) * HEAD)
+
+
+def span_kernel(
+    deep, q_hbm, kv_hbm, cur_pos_ref, cache_ref, cache_pos_ref, count_ref, visible_ref, out_ref,
+    q_raw, kv_raw, q_rot, k_rot, cos_ref, sin_ref, keys, values, bias_ref, load_sem, own_sem,
+    send_sem, recv_sem,
+):
+    me = lax.axis_index("tm")
+    place = me // LANE
+    column = (me % LANE) // CORES
+    core = me % CORES
+    slots = cache_ref.shape[1]
+    depth = cache_ref.shape[2]
+    blocks = deep * LANE
+    scale = HEAD ** (-0.5)
+    core_other = me + 1 - 2 * core
+    column_other = me + CORES - 2 * CORES * column
+    barrier = pltpu.get_barrier_semaphore()
+
+    def greet(device):
+        pl.semaphore_signal(
+            barrier, inc=1, device_id={"tm": device}, device_id_type=pl.DeviceIdType.MESH
+        )
+
+    greet(core_other)
+    greet(column_other)
+    pl.when(place > 0)(lambda: greet(me - LANE))
+    pl.when(place < deep - 1)(lambda: greet(me + LANE))
+
+    load_q = pltpu.make_async_copy(q_hbm, q_raw, load_sem.at[0])
+    load_kv = pltpu.make_async_copy(kv_hbm, kv_raw, load_sem.at[1])
+    own_values = pltpu.make_async_copy(cache_ref.at[1], values.at[me], own_sem)
+    load_q.start()
+    load_kv.start()
+    own_values.start()
+
+    cosine, sine = turn_tables(cache_pos_ref[0:1, :], cache_pos_ref[1:2, :], cache_pos_ref[2:3, :])
+    for h in range(HEADS):
+        keys[me, :, head_columns(h)] = turn(cache_ref[0, :, head_columns(h)], cosine, sine)
+    row = lax.broadcasted_iota(jnp.int32, (slots, HEAD), 0)
+    keys[me, :, depth:] = jnp.where(row < count_ref[0, 0], 0.0, masked_value).astype(jnp.bfloat16)
+
+    pl.semaphore_wait(
+        barrier,
+        2 + (place > 0).astype(jnp.int32) + (place < deep - 1).astype(jnp.int32),
+    )
+
+    def message(part, slot, direction, device, own=False):
+        buffer = (values, keys)[part]
+        source = cache_ref.at[1] if own and part == 0 else buffer.at[slot]
+        return pltpu.make_async_remote_copy(
+            src_ref=source,
+            dst_ref=buffer.at[slot],
+            send_sem=send_sem.at[part, slot, direction],
+            recv_sem=recv_sem.at[part, slot],
+            device_id={"tm": device},
+            device_id_type=pl.DeviceIdType.MESH,
+        )
+
+    def arrived(part, slot):
+        message(part, slot, 0, core_other).wait_recv()
+
+    def upward(part, slot, own=False):
+        return message(part, slot, 0, me + LANE, own)
+
+    def downward(part, slot, own=False):
+        return message(part, slot, 1, me - LANE, own)
+
+    def across(part, slot, own=False):
+        return message(part, slot, 2, column_other, own)
+
+    def over(part, slot, own=False):
+        return message(part, slot, 3, core_other, own)
+
+    for part in range(2):
+        pl.when(place < deep - 1)(lambda: upward(part, me, True).start())
+        pl.when(place > 0)(lambda: downward(part, me, True).start())
+        across(part, me, True).start()
+        over(part, me, True).start()
+
+    def line(distance, part):
+        @pl.when(place >= distance)
+        def _():
+            slot = me - distance * LANE
+            arrived(part, slot)
+            pl.when(place < deep - 1)(lambda: upward(part, slot).start())
+            across(part, slot).start()
+            over(part, slot).start()
+
+        @pl.when(place < deep - distance)
+        def _():
+            slot = me + distance * LANE
+            arrived(part, slot)
+            pl.when(place > 0)(lambda: downward(part, slot).start())
+            across(part, slot).start()
+            over(part, slot).start()
+
+    def side(distance, part):
+        def relay(slot):
+            arrived(part, slot)
+            over(part, slot).start()
+
+        if distance == 0:
+            relay(column_other)
+        else:
+            pl.when(place >= distance)(lambda: relay(column_other - distance * LANE))
+            pl.when(place < deep - distance)(lambda: relay(column_other + distance * LANE))
+
+    load_q.wait()
+    load_kv.wait()
+    queries = q_raw.shape[0]
+    span_rows = cur_pos_ref.shape[1]
+    width = cur_pos_ref.shape[2]
+    for r in range(span_rows):
+        cosine, sine = turn_tables(
+            cur_pos_ref[0, r : r + 1, :], cur_pos_ref[1, r : r + 1, :], cur_pos_ref[2, r : r + 1, :]
+        )
+        cos_ref[r * width : (r + 1) * width, :] = cosine
+        sin_ref[r * width : (r + 1) * width, :] = sine
+
+    def turn_current(first, last):
+        for h in range(first, last):
+            q_rot[:, head_columns(h)] = turn(q_raw[:, head_columns(h)], cos_ref[...], sin_ref[...])
+            k_rot[:, head_columns(h)] = turn(
+                kv_raw[0, :, head_columns(h)], cos_ref[...], sin_ref[...]
+            )
+
+    turn_current(0, HEADS)
+    for distance in range(1, deep):
+        for part in range(2):
+            line(distance, part)
+        for part in range(2):
+            side(distance - 1, part)
+    for part in range(2):
+        side(deep - 1, part)
+    for far in range(deep):
+        for c in range(COLUMNS):
+            for part in range(2):
+                arrived(part, far * LANE + c * CORES + 1 - core)
+    own_values.wait()
+
+    for e in range(blocks):
+        seen = jnp.where(visible_ref[0, e] > 0, 0.0, masked_value)
+        bias_ref[e * slots : (e + 1) * slots, :] = jnp.minimum(
+            keys[e, :, depth:].astype(jnp.float32), seen
+        ).astype(jnp.bfloat16)
+    pick = (lax.broadcasted_iota(jnp.int32, (16, HEAD), 1) == 0).astype(jnp.float32)
+    bias = lax.dot_general(
+        pick.astype(jnp.bfloat16), bias_ref[...], (((1,), (1,)), ((), ())),
+        preferred_element_type=jnp.float32,
+    )[0:1, :]
+    for h in range(HEADS):
+        cols = head_columns(h)
+        q = q_rot[:, cols]
+        near = lax.dot_general(
+            q, k_rot[:, cols], (((1,), (1,)), ((), ())), preferred_element_type=jnp.float32
+        ) * scale
+        far = lax.dot_general(
+            q, keys[:, :, cols].reshape(blocks * slots, HEAD), (((1,), (1,)), ((), ())),
+            preferred_element_type=jnp.float32,
+        ) * scale + bias
+        highest = jnp.maximum(
+            jnp.max(near, axis=-1, keepdims=True), jnp.max(far, axis=-1, keepdims=True)
+        )
+        near = jnp.exp(near - highest)
+        far = jnp.exp(far - highest)
+        total = jnp.sum(near, axis=-1, keepdims=True) + jnp.sum(far, axis=-1, keepdims=True)
+        summed = jnp.dot(
+            near.astype(jnp.bfloat16), kv_raw[1, :, cols], preferred_element_type=jnp.float32
+        ) + jnp.dot(
+            far.astype(jnp.bfloat16), values[:, :, cols].reshape(blocks * slots, HEAD),
+            preferred_element_type=jnp.float32,
+        )
+        out_ref[:, cols] = (summed / total).astype(jnp.bfloat16)
+
+    def sent(slot, own=False):
+        for part in range(2):
+            across(part, slot, own).wait_send()
+            over(part, slot, own).wait_send()
+
+    for part in range(2):
+        pl.when(place < deep - 1)(lambda: upward(part, me, True).wait_send())
+        pl.when(place > 0)(lambda: downward(part, me, True).wait_send())
+    sent(me, True)
+    for part in range(2):
+        over(part, column_other).wait_send()
+    for distance in range(1, deep):
+        @pl.when(place >= distance)
+        def _():
+            slot = me - distance * LANE
+            sent(slot)
+            for part in range(2):
+                pl.when(place < deep - 1)(lambda: upward(part, slot).wait_send())
+                over(part, column_other - distance * LANE).wait_send()
+
+        @pl.when(place < deep - distance)
+        def _():
+            slot = me + distance * LANE
+            sent(slot)
+            for part in range(2):
+                pl.when(place > 0)(lambda: downward(part, slot).wait_send())
+                over(part, column_other + distance * LANE).wait_send()
+
+
+def whole_rows(query, cur_kv, cur_pos, cache_kv, cache_pos, counts, visible):
+    frames, tile_rows, columns, depth = query.shape
+    queries = tile_rows * columns
+    slots = cache_kv.shape[2]
+    deep = lax.axis_size("tm") // LANE
+    blocks = deep * LANE
+    vmem = pl.BlockSpec(memory_space=pltpu.VMEM)
+    smem = pl.BlockSpec(memory_space=pltpu.SMEM)
+    hbm = pl.BlockSpec(memory_space=pl.ANY)
+    output = pl.pallas_call(
+        lambda *refs: span_kernel(deep, *refs),
+        out_shape=jax.ShapeDtypeStruct((queries, depth), jnp.bfloat16),
+        in_specs=[hbm, hbm, vmem, vmem, vmem, smem, smem],
+        out_specs=vmem,
+        scratch_shapes=[
+            pltpu.VMEM((queries, depth), jnp.bfloat16),
+            pltpu.VMEM((2, queries, depth), jnp.bfloat16),
+            pltpu.VMEM((queries, depth), jnp.bfloat16),
+            pltpu.VMEM((queries, depth), jnp.bfloat16),
+            pltpu.VMEM((queries, HEAD), jnp.float32),
+            pltpu.VMEM((queries, HEAD), jnp.float32),
+            pltpu.VMEM((blocks, slots, depth + HEAD), jnp.bfloat16),
+            pltpu.VMEM((blocks, slots, depth), jnp.bfloat16),
+            pltpu.VMEM((blocks * slots, HEAD), jnp.bfloat16),
+            pltpu.SemaphoreType.DMA((2,)),
+            pltpu.SemaphoreType.DMA,
+            pltpu.SemaphoreType.DMA((2, blocks, DIRECTIONS)),
+            pltpu.SemaphoreType.DMA((2, blocks)),
+        ],
+        compiler_params=pltpu.CompilerParams(collective_id=0, has_side_effects=True),
+    )(
+        query.reshape(queries, depth),
+        cur_kv.reshape(2, queries, depth),
+        cur_pos.reshape(3, tile_rows, columns),
+        cache_kv.reshape(2, slots, depth),
+        cache_pos.reshape(3, slots),
+        counts,
+        visible,
+    )
+    return output.reshape(frames, tile_rows, columns, depth)
+
+
+def span_attention(query, *rest):
+    fits = (
+        lax.axis_size("height") == 1
+        and query.shape[0] == 1
+        and query.shape[1] <= REACH + 1
+        and lax.axis_size("tm") % LANE == 0
+    )
+    return (whole_rows if fits else per_device)(query, *rest)
+
+
 def solution(mesh):
     in_specs = (
         P(("group", "tm"), "height", None, None),
@@ -147,5 +451,5 @@
     )
     out_specs = P(("group", "tm"), "height", None, None)
     return jax.shard_map(
-        per_device, mesh=mesh, in_specs=in_specs, out_specs=out_specs, check_vma=False
-    )
+        span_attention, mesh=mesh, in_specs=in_specs, out_specs=out_specs, check_vma=False
+    )

time: 137 us -> 35.1 us (0.26)
  local copies, waits for them, and re-layouts: 44 us -> 3.02 us
  other arithmetic: 36.1 us -> 0 us
  blocking collectives: 32.2 us -> 0 us
  Pallas kernels: 0 us -> 31.2 us
  between operations: 14.4 us -> 0.67 us
  matrix products: 7.29 us -> 0 us
  starting transfers between devices: 1.67 us -> 0 us
    pallas_call x0 -> x1, Pallas kernels: none -> 31.2 us  [whole_rows(): pl.pallas_call(lambda *refs: span_kernel(deep, *refs), out_shape=jax.Shap...]
    another operation x6 -> x0, other arithmetic: 24.7 us -> none  [the longest x3 12.5 us: rotate(): jnp.stack([lower * cosine - upper * sine, upper * cosine + lower * sine],...]
    all_gather x1 -> x0, blocking collectives: 20.5 us -> none  [per_device(): position_piece = lax.all_gather(cache_pos, 'tm', axis=0, tiled=True)]
    slice x3 -> x0, local copies, waits for them, and re-layouts: 16.4 us -> none  [the longest x2 15.2 us: rotate(): lower = shaped[..., 0, :]]
    unnamed x1 -> x0, blocking collectives: 11.6 us -> none
    convert_element_type x5 -> x0, local copies, waits for them, and re-layouts: 10.3 us -> none  [the longest x2 6.85 us: rotate(): vectors.astype(jnp.float32)]
    another operation x4 -> x0, local copies, waits for them, and re-layouts: 8.87 us -> none  [the longest x1 4.01 us: per_device(): pair_piece[:, 1].reshape(blocks * slots, HEADS, HEAD)]
    dot_general x4 -> x0, matrix products: 7.29 us -> none  [the longest x1 2.75 us: per_device(): jnp.einsum('fhqk,fhkd->fhqd', weights.astype(jnp.bfloat16), local_values,...]
  transfers between devices with their start and end apart: 2 -> 0, of which waited for: 0 -> 0; matrix products, arithmetic and copies ran while one was open for 23% -> 0% of each run, Pallas kernels for 0% -> 0%
where the time goes in v1:
time: 35.1 us; the launch traced here: 34.9 us
  Pallas kernels  31.2 us (89%)
  local copies, waits for them, and re-layouts  3.02 us (9%)
  between operations  0.67 us (2%)
    pallas_call x1, Pallas kernels, whole_rows(): pl.pallas_call(lambda *refs: span_kernel(deep, *refs), out_shape=jax.Shap...  31.2 us
    unnamed x4, local copies, waits for them, and re-layouts  3.02 us

profile of v1, /device:TPU:1, one launch (start us, length us, event | category | flops | bytes accessed | tf_op | source)
XLA Modules:
  0.0 34.9 jit_solution(15673592756591093525)
XLA Ops:
  0.7 0.0 copy-start
  0.7 0.7 %copy-done = s32[1,3,32]{2,0,1:T(1,128)S(1)} copy-done((s32[1,3,32]{2,0,1:T(1,128)S(1)}, s32[1,3,32]{2,0,1:T(1,128)}, u32[]{:S(2)}) %copy-start) | copy-done | bytes 408
  1.3 0.6 %copy.10 = s32[1,3,32]{2,1,0:T(4,128)} copy(s32[1,3,32]{2,0,1:T(1,128)S(1)} %copy-done) | data formatting | bytes 768
  1.9 31.2 %shard_map.73 = bf16[128,1536]{1,0:T(8,128)(2,1)} custom-call(bf16[128,1536]{1,0:T(8,128)(2,1)} %bitcast.10, bf16[2,128,1536]{2,1,0:T(8,128)(2,1)} %bitcast.9, s32[3,2,64]{2,1,0:T(2,128)} %bitcast.13, bf16[2,32,1536]{2,1,0:T(8,128)(2,1)} %bitcast.11, s32[3,32]{1,0:T(4,128)} %bitcast.12, s32[1,1]{1,0:T(1,128)S(6)} %copy.12.refs_5_, s32[1,16]{1,0:T(1,128)} %refs_6_.1), custom_call_target="tpu_custom_call" | custom-call | tf_op jit(solution)/shard_map/pallas_call | solution.py:399
  33.1 1.8 %copy.13 = bf16[1,2,64,1536]{3,2,1,0:T(8,128)(2,1)} copy(bf16[1,2,64,1536]{3,2,1,0:T(8,128)(2,1)} %bitcast.8) | data formatting | bytes 786432
Async XLA Ops:
  0.7 0.7 %copy-start = (s32[1,3,32]{2,0,1:T(1,128)S(1)}, s32[1,3,32]{2,0,1:T(1,128)}, u32[]{:S(2)}) copy-start(s32[1,3,32]{2,0,1:T(1,128)} %param.11) | copy-start | bytes 1156

commit v2 on v1

--- a/solution.py
+++ b/solution.py
@@ -181,13 +181,18 @@
     return (wide * cosine + pltpu.roll(wide, HEAD // 2, 1) * sine).astype(jnp.bfloat16)
 
 
+def fold(weights):
+    pieces = [weights[:, i : i + HEAD] for i in range(0, weights.shape[1], HEAD)]
+    return sum(pieces[1:], pieces[0])
+
+
 def head_columns(h):
     return slice(h * HEAD, (h + 1) * HEAD)
 
 
 def span_kernel(
-    deep, q_hbm, kv_hbm, cur_pos_ref, cache_ref, cache_pos_ref, count_ref, visible_ref, out_ref,
-    q_raw, kv_raw, q_rot, k_rot, cos_ref, sin_ref, keys, values, bias_ref, load_sem, own_sem,
+    deep, q_hbm, kv_hbm, cur_pos_ref, cache_ref, cache_pos_hbm, count_ref, visible_ref, out_ref,
+    q_raw, kv_raw, q_rot, k_rot, cos_ref, sin_ref, keys, values, kept_pos, top_ref, total_ref, sum_ref, load_sem, own_sem,
     send_sem, recv_sem,
 ):
     me = lax.axis_index("tm")
@@ -207,6 +212,8 @@
             barrier, inc=1, device_id={"tm": device}, device_id_type=pl.DeviceIdType.MESH
         )
 
+    load_pos = pltpu.make_async_copy(cache_pos_hbm, kept_pos, load_sem.at[2])
+    load_pos.start()
     greet(core_other)
     greet(column_other)
     pl.when(place > 0)(lambda: greet(me - LANE))
@@ -219,7 +226,8 @@
     load_kv.start()
     own_values.start()
 
-    cosine, sine = turn_tables(cache_pos_ref[0:1, :], cache_pos_ref[1:2, :], cache_pos_ref[2:3, :])
+    load_pos.wait()
+    cosine, sine = turn_tables(kept_pos[0], kept_pos[1], kept_pos[2])
     for h in range(HEADS):
         keys[me, :, head_columns(h)] = turn(cache_ref[0, :, head_columns(h)], cosine, sine)
     row = lax.broadcasted_iota(jnp.int32, (slots, HEAD), 0)
@@ -311,52 +319,80 @@
             )
 
     turn_current(0, HEADS)
+    pick = (lax.broadcasted_iota(jnp.int32, (16, HEAD), 1) == 0).astype(jnp.float32)
+    pick = pick.astype(jnp.bfloat16)
+    transposed = (((1,), (1,)), ((), ()))
+    for h in range(HEADS):
+        cols = head_columns(h)
+        scores = lax.dot_general(
+            q_rot[:, cols], k_rot[:, cols], transposed, preferred_element_type=jnp.float32
+        ) * scale
+        highest = jnp.max(scores, axis=-1, keepdims=True)
+        weights = jnp.exp(scores - highest)
+        top_ref[:, cols] = jnp.broadcast_to(highest, (queries, HEAD))
+        total_ref[:, cols] = fold(weights)
+        sum_ref[:, cols] = jnp.dot(
+            weights.astype(jnp.bfloat16), kv_raw[1, :, cols], preferred_element_type=jnp.float32
+        )
+
+    def plane(number, last):
+        first = number * LANE
+        for c in range(COLUMNS):
+            for part in range(2):
+                arrived(part, first + c * CORES + 1 - core)
+        spans = []
+        for i in range(LANE):
+            seen = jnp.where(visible_ref[0, first + i] > 0, 0.0, masked_value)
+            spans.append(
+                jnp.minimum(keys[first + i, :, depth:].astype(jnp.float32), seen)
+            )
+        bias = lax.dot_general(
+            pick, jnp.concatenate(spans, axis=0).astype(jnp.bfloat16), transposed,
+            preferred_element_type=jnp.float32,
+        )[0:1, :]
+        for h in range(HEADS):
+            cols = head_columns(h)
+            block = keys[pl.ds(first, LANE), :, cols].reshape(LANE * slots, HEAD)
+            scores = lax.dot_general(
+                q_rot[:, cols], block, transposed, preferred_element_type=jnp.float32
+            ) * scale + bias
+            old = top_ref[:, cols]
+            highest = jnp.maximum(old, jnp.max(scores, axis=-1, keepdims=True))
+            fading = jnp.exp(old - highest)
+            weights = jnp.exp(scores - highest[:, 0:1])
+            total = total_ref[:, cols] * fading + fold(weights)
+            summed = sum_ref[:, cols] * fading + jnp.dot(
+                weights.astype(jnp.bfloat16),
+                values[pl.ds(first, LANE), :, cols].reshape(LANE * slots, HEAD),
+                preferred_element_type=jnp.float32,
+            )
+            if last:
+                out_ref[:, cols] = (
+                    summed / jnp.sum(total, axis=-1, keepdims=True)
+                ).astype(jnp.bfloat16)
+            else:
+                top_ref[:, cols] = highest
+                total_ref[:, cols] = total
+                sum_ref[:, cols] = summed
+
+    nearest = [sorted(range(deep), key=lambda other: abs(other - z)) for z in range(deep)]
+
+    def ordered(k):
+        number = 0
+        for z in range(deep):
+            number = number + (place == z).astype(jnp.int32) * nearest[z][k]
+        return number
+
+    own_values.wait()
     for distance in range(1, deep):
         for part in range(2):
             line(distance, part)
         for part in range(2):
             side(distance - 1, part)
+        plane(ordered(distance - 1), False)
     for part in range(2):
         side(deep - 1, part)
-    for far in range(deep):
-        for c in range(COLUMNS):
-            for part in range(2):
-                arrived(part, far * LANE + c * CORES + 1 - core)
-    own_values.wait()
-
-    for e in range(blocks):
-        seen = jnp.where(visible_ref[0, e] > 0, 0.0, masked_value)
-        bias_ref[e * slots : (e + 1) * slots, :] = jnp.minimum(
-            keys[e, :, depth:].astype(jnp.float32), seen
-        ).astype(jnp.bfloat16)
-    pick = (lax.broadcasted_iota(jnp.int32, (16, HEAD), 1) == 0).astype(jnp.float32)
-    bias = lax.dot_general(
-        pick.astype(jnp.bfloat16), bias_ref[...], (((1,), (1,)), ((), ())),
-        preferred_element_type=jnp.float32,
-    )[0:1, :]
-    for h in range(HEADS):
-        cols = head_columns(h)
-        q = q_rot[:, cols]
-        near = lax.dot_general(
-            q, k_rot[:, cols], (((1,), (1,)), ((), ())), preferred_element_type=jnp.float32
-        ) * scale
-        far = lax.dot_general(
-            q, keys[:, :, cols].reshape(blocks * slots, HEAD), (((1,), (1,)), ((), ())),
-            preferred_element_type=jnp.float32,
-        ) * scale + bias
-        highest = jnp.maximum(
-            jnp.max(near, axis=-1, keepdims=True), jnp.max(far, axis=-1, keepdims=True)
-        )
-        near = jnp.exp(near - highest)
-        far = jnp.exp(far - highest)
-        total = jnp.sum(near, axis=-1, keepdims=True) + jnp.sum(far, axis=-1, keepdims=True)
-        summed = jnp.dot(
-            near.astype(jnp.bfloat16), kv_raw[1, :, cols], preferred_element_type=jnp.float32
-        ) + jnp.dot(
-            far.astype(jnp.bfloat16), values[:, :, cols].reshape(blocks * slots, HEAD),
-            preferred_element_type=jnp.float32,
-        )
-        out_ref[:, cols] = (summed / total).astype(jnp.bfloat16)
+    plane(ordered(deep - 1), True)
 
     def sent(slot, own=False):
         for part in range(2):
@@ -395,11 +431,11 @@
     blocks = deep * LANE
     vmem = pl.BlockSpec(memory_space=pltpu.VMEM)
     smem = pl.BlockSpec(memory_space=pltpu.SMEM)
-    hbm = pl.BlockSpec(memory_space=pl.ANY)
+    hbm = pl.BlockSpec(memory_space=pltpu.HBM)
     output = pl.pallas_call(
         lambda *refs: span_kernel(deep, *refs),
         out_shape=jax.ShapeDtypeStruct((queries, depth), jnp.bfloat16),
-        in_specs=[hbm, hbm, vmem, vmem, vmem, smem, smem],
+        in_specs=[hbm, hbm, vmem, vmem, hbm, smem, smem],
         out_specs=vmem,
         scratch_shapes=[
             pltpu.VMEM((queries, depth), jnp.bfloat16),
@@ -410,19 +446,24 @@
             pltpu.VMEM((queries, HEAD), jnp.float32),
             pltpu.VMEM((blocks, slots, depth + HEAD), jnp.bfloat16),
             pltpu.VMEM((blocks, slots, depth), jnp.bfloat16),
-            pltpu.VMEM((blocks * slots, HEAD), jnp.bfloat16),
-            pltpu.SemaphoreType.DMA((2,)),
+            pltpu.VMEM((3, 1, slots), jnp.int32),
+            pltpu.VMEM((queries, depth), jnp.float32),
+            pltpu.VMEM((queries, depth), jnp.float32),
+            pltpu.VMEM((queries, depth), jnp.float32),
+            pltpu.SemaphoreType.DMA((3,)),
             pltpu.SemaphoreType.DMA,
             pltpu.SemaphoreType.DMA((2, blocks, DIRECTIONS)),
             pltpu.SemaphoreType.DMA((2, blocks)),
         ],
-        compiler_params=pltpu.CompilerParams(collective_id=0, has_side_effects=True),
+        compiler_params=pltpu.CompilerParams(
+            collective_id=0, has_side_effects=True, vmem_limit_bytes=24 * 1024 * 1024
+        ),
     )(
         query.reshape(queries, depth),
         cur_kv.reshape(2, queries, depth),
         cur_pos.reshape(3, tile_rows, columns),
         cache_kv.reshape(2, slots, depth),
-        cache_pos.reshape(3, slots),
+        jnp.transpose(cache_pos, (1, 0, 2)),
         counts,
         visible,
     )
@@ -434,6 +475,7 @@
         lax.axis_size("height") == 1
         and query.shape[0] == 1
         and query.shape[1] <= REACH + 1
+        and query.shape[1] * query.shape[2] % HEAD == 0
         and lax.axis_size("tm") % LANE == 0
     )
     return (whole_rows if fits else per_device)(query, *rest)

time: 35.1 us -> 39 us (1.11)
  Pallas kernels: 31.2 us -> 33.6 us
  local copies, waits for them, and re-layouts: 3.02 us -> 4.48 us
    pallas_call x1, Pallas kernels: 31.2 us -> 33.6 us  [whole_rows(): pl.pallas_call(lambda *refs: span_kernel(deep, *refs), out_shape=jax.Shap...]
    unnamed x4 -> x13, local copies, waits for them, and re-layouts: 3.02 us -> 4.48 us
where the time goes in v2:
time: 39 us; the launch traced here: 38.8 us
  Pallas kernels  33.6 us (86%)
  local copies, waits for them, and re-layouts  4.48 us (11%)
  between operations  0.69 us (2%)
    pallas_call x1, Pallas kernels, whole_rows(): pl.pallas_call(lambda *refs: span_kernel(deep, *refs), out_shape=jax.Shap...  33.6 us
    unnamed x13, local copies, waits for them, and re-layouts  4.48 us

profile of v2, /device:TPU:1, one launch (start us, length us, event | category | flops | bytes accessed | tf_op | source)
XLA Modules:
  0.0 38.8 jit_solution(6556355839993923611)
XLA Ops:
  0.7 0.0 copy-start.3
  0.7 0.0 copy-start.4
  0.7 0.0 copy-start.5
  0.7 0.7 %copy-done.3 = s32[3,1,2,64]{3,2,1,0:T(2,128)S(1)} copy-done((s32[3,1,2,64]{3,2,1,0:T(2,128)S(1)}, s32[3,1,2,64]{3,2,1,0:T(2,128)}, u32[]{:S(2)}) %copy-start.3) | copy-done | bytes 1560
  1.3 0.0 copy-done.4
  1.3 0.0 copy-done.5
  1.4 0.0 copy-start
  1.4 1.1 %copy-done = bf16[2,1,2,64,1536]{4,3,2,1,0:T(8,128)(2,1)S(1)} copy-done((bf16[2,1,2,64,1536]{4,3,2,1,0:T(8,128)(2,1)S(1)}, bf16[2,1,2,64,1536]{4,3,2,1,0:T(8,128)(2,1)}, u32[]{:S(2)}) %copy-start) | copy-done | bytes 786456
  2.5 0.0 copy-start.1
  2.5 1.0 %copy-done.1 = bf16[1,2,64,1536]{3,2,1,0:T(8,128)(2,1)S(1)} copy-done((bf16[1,2,64,1536]{3,2,1,0:T(8,128)(2,1)S(1)}, bf16[1,2,64,1536]{3,2,1,0:T(8,128)(2,1)}, u32[]{:S(2)}) %copy-start.1) | copy-done | bytes 393240
  3.5 0.0 copy-start.2
  3.5 0.9 %copy-done.2 = bf16[1,2,32,1536]{3,2,1,0:T(8,128)(2,1)S(1)} copy-done((bf16[1,2,32,1536]{3,2,1,0:T(8,128)(2,1)S(1)}, bf16[1,2,32,1536]{3,2,1,0:T(8,128)(2,1)}, u32[]{:S(2)}) %copy-start.2) | copy-done | bytes 196632
  4.4 33.6 %shard_map.73 = bf16[128,1536]{1,0:T(8,128)(2,1)S(1)} custom-call(bf16[128,1536]{1,0:T(8,128)(2,1)S(1)} %bitcast.8, bf16[2,128,1536]{2,1,0:T(8,128)(2,1)S(1)} %bitcast.7, s32[3,2,64]{2,1,0:T(2,128)S(1)} %bitcast.10, bf16[2,32,1536]{2,1,0:T(8,128)(2,1)S(1)} %bitcast.9, s32[3,1,32]{2,1,0:T(1,128)S(1)} %bitcast.11, s32[1,1]{1,0:T(1,128)S(6)} %copy.9.refs_5_, ...), custom_call_target="tpu_custom_call" | custom-call | tf_op jit(solution)/shard_map/pallas_call | solution.py:435
  38.0 0.7 %copy.10 = bf16[1,2,64,1536]{3,2,1,0:T(8,128)(2,1)} copy(bf16[1,2,64,1536]{3,2,1,0:T(8,128)(2,1)S(1)} %bitcast.6) | data formatting | bytes 786432
Async XLA Ops:
  0.7 0.7 %copy-start.3 = (s32[3,1,2,64]{3,2,1,0:T(2,128)S(1)}, s32[3,1,2,64]{3,2,1,0:T(2,128)}, u32[]{:S(2)}) copy-start(s32[3,1,2,64]{3,2,1,0:T(2,128)} %param.9) | copy-start | bytes 4612
  0.7 0.7 %copy-start.4 = (s32[1,3,32]{2,0,1:T(1,128)S(1)}, s32[1,3,32]{2,0,1:T(1,128)}, u32[]{:S(2)}) copy-start(s32[1,3,32]{2,0,1:T(1,128)} %param.11) | copy-start | bytes 1156
  0.7 0.7 %copy-start.5 = (s32[1,16]{1,0:T(1,128)S(1)}, s32[1,16]{1,0:T(1,128)}, u32[]{:S(2)}) copy-start(s32[1,16]{1,0:T(1,128)} %refs_6_.1) | copy-start | bytes 196
  1.4 1.1 %copy-start = (bf16[2,1,2,64,1536]{4,3,2,1,0:T(8,128)(2,1)S(1)}, bf16[2,1,2,64,1536]{4,3,2,1,0:T(8,128)(2,1)}, u32[]{:S(2)}) copy-start(bf16[2,1,2,64,1536]{4,3,2,1,0:T(8,128)(2,1)} %param.8) | copy-start | bytes 2359300
  2.5 1.0 %copy-start.1 = (bf16[1,2,64,1536]{3,2,1,0:T(8,128)(2,1)S(1)}, bf16[1,2,64,1536]{3,2,1,0:T(8,128)(2,1)}, u32[]{:S(2)}) copy-start(bf16[1,2,64,1536]{3,2,1,0:T(8,128)(2,1)} %param.7) | copy-start | bytes 1179652
  3.5 0.9 %copy-start.2 = (bf16[1,2,32,1536]{3,2,1,0:T(8,128)(2,1)S(1)}, bf16[1,2,32,1536]{3,2,1,0:T(8,128)(2,1)}, u32[]{:S(2)}) copy-start(bf16[1,2,32,1536]{3,2,1,0:T(8,128)(2,1)} %param.10) | copy-start | bytes 589828

commit v3 on v2

--- a/solution.py
+++ b/solution.py
@@ -192,7 +192,7 @@
 
 def span_kernel(
     deep, q_hbm, kv_hbm, cur_pos_ref, cache_ref, cache_pos_hbm, count_ref, visible_ref, out_ref,
-    q_raw, kv_raw, q_rot, k_rot, cos_ref, sin_ref, keys, values, kept_pos, top_ref, total_ref, sum_ref, load_sem, own_sem,
+    q_raw, kv_raw, q_rot, k_rot, cos_ref, sin_ref, keys, values, kept_pos, top_ref, total_ref, sum_ref, bias_ref, load_sem, own_sem,
     send_sem, recv_sem,
 ):
     me = lax.axis_index("tm")
@@ -322,20 +322,21 @@
     pick = (lax.broadcasted_iota(jnp.int32, (16, HEAD), 1) == 0).astype(jnp.float32)
     pick = pick.astype(jnp.bfloat16)
     transposed = (((1,), (1,)), ((), ()))
-    for h in range(HEADS):
-        cols = head_columns(h)
-        scores = lax.dot_general(
-            q_rot[:, cols], k_rot[:, cols], transposed, preferred_element_type=jnp.float32
-        ) * scale
-        highest = jnp.max(scores, axis=-1, keepdims=True)
-        weights = jnp.exp(scores - highest)
-        top_ref[:, cols] = jnp.broadcast_to(highest, (queries, HEAD))
-        total_ref[:, cols] = fold(weights)
-        sum_ref[:, cols] = jnp.dot(
-            weights.astype(jnp.bfloat16), kv_raw[1, :, cols], preferred_element_type=jnp.float32
-        )
-
-    def plane(number, last):
+    def near_attention():
+        for h in range(HEADS):
+            cols = head_columns(h)
+            scores = lax.dot_general(
+                q_rot[:, cols], k_rot[:, cols], transposed, preferred_element_type=jnp.float32
+            ) * scale
+            highest = jnp.max(scores, axis=-1, keepdims=True)
+            weights = jnp.exp(scores - highest)
+            top_ref[:, cols] = jnp.broadcast_to(highest, (queries, HEAD))
+            total_ref[:, cols] = fold(weights)
+            sum_ref[:, cols] = jnp.dot(
+                weights.astype(jnp.bfloat16), kv_raw[1, :, cols], preferred_element_type=jnp.float32
+            )
+
+    def gather(number):
         first = number * LANE
         for c in range(COLUMNS):
             for part in range(2):
@@ -346,11 +347,15 @@
             spans.append(
                 jnp.minimum(keys[first + i, :, depth:].astype(jnp.float32), seen)
             )
-        bias = lax.dot_general(
+        bias_ref[...] = lax.dot_general(
             pick, jnp.concatenate(spans, axis=0).astype(jnp.bfloat16), transposed,
             preferred_element_type=jnp.float32,
-        )[0:1, :]
-        for h in range(HEADS):
+        )
+
+    def plane(number, start, stop, last):
+        first = number * LANE
+        bias = bias_ref[0:1, :]
+        for h in range(start, stop):
             cols = head_columns(h)
             block = keys[pl.ds(first, LANE), :, cols].reshape(LANE * slots, HEAD)
             scores = lax.dot_general(
@@ -384,15 +389,27 @@
         return number
 
     own_values.wait()
+    half = HEADS // 2
+    number = None
     for distance in range(1, deep):
         for part in range(2):
             line(distance, part)
-        for part in range(2):
             side(distance - 1, part)
-        plane(ordered(distance - 1), False)
+            if distance == 1 and part == 0:
+                near_attention()
+                continue
+            if part == 0:
+                plane(number, half, HEADS, False)
+            else:
+                number = ordered(distance - 1)
+                gather(number)
+                plane(number, 0, half, False)
+    plane(number, half, HEADS, False)
     for part in range(2):
         side(deep - 1, part)
-    plane(ordered(deep - 1), True)
+    number = ordered(deep - 1)
+    gather(number)
+    plane(number, 0, HEADS, True)
 
     def sent(slot, own=False):
         for part in range(2):
@@ -450,14 +467,13 @@
             pltpu.VMEM((queries, depth), jnp.float32),
             pltpu.VMEM((queries, depth), jnp.float32),
             pltpu.VMEM((queries, depth), jnp.float32),
+            pltpu.VMEM((16, LANE * slots), jnp.float32),
             pltpu.SemaphoreType.DMA((3,)),
             pltpu.SemaphoreType.DMA,
             pltpu.SemaphoreType.DMA((2, blocks, DIRECTIONS)),
             pltpu.SemaphoreType.DMA((2, blocks)),
         ],
-        compiler_params=pltpu.CompilerParams(
-            collective_id=0, has_side_effects=True, vmem_limit_bytes=24 * 1024 * 1024
-        ),
+        compiler_params=pltpu.CompilerParams(collective_id=0, has_side_effects=True),
     )(
         query.reshape(queries, depth),
         cur_kv.reshape(2, queries, depth),

time: 39 us -> 36.7 us (0.941)
  the two profiles are of different devices: /device:TPU:1 before, /device:TPU:0 now
where the time goes in v3:
time: 36.7 us; the launch traced here: 36.5 us
  Pallas kernels  34.1 us (93%)
  local copies, waits for them, and re-layouts  1.77 us (5%)
  between operations  0.66 us (2%)
    pallas_call x1, Pallas kernels, whole_rows(): pl.pallas_call(lambda *refs: span_kernel(deep, *refs), out_shape=jax.Shap...  34.1 us
    unnamed x1, local copies, waits for them, and re-layouts  1.77 us

profile of v3, /device:TPU:0, one launch (start us, length us, event | category | flops | bytes accessed | tf_op | source)
XLA Modules:
  0.0 36.5 jit_solution(4548788581684935598)
XLA Ops:
  0.7 34.1 %shard_map.73 = bf16[128,1536]{1,0:T(8,128)(2,1)} custom-call(bf16[128,1536]{1,0:T(8,128)(2,1)} %bitcast.8, bf16[2,128,1536]{2,1,0:T(8,128)(2,1)} %bitcast.7, s32[3,2,64]{2,1,0:T(2,128)} %bitcast.10, bf16[2,32,1536]{2,1,0:T(8,128)(2,1)} %bitcast.9, s32[3,1,32]{2,1,0:T(1,128)} %bitcast.11, s32[1,1]{1,0:T(1,128)S(6)} %copy.9.refs_5_, s32[1,16]{1,0:T(1,128)} %refs_6_.1), custom_call_target="tpu_custom_call" | custom-call | tf_op jit(solution)/shard_map/pallas_call | solution.py:452
  34.7 1.8 %copy.10 = bf16[1,2,64,1536]{3,2,1,0:T(8,128)(2,1)} copy(bf16[1,2,64,1536]{3,2,1,0:T(8,128)(2,1)} %bitcast.6) | data formatting | bytes 786432

commit v4 on v3

--- a/solution.py
+++ b/solution.py
@@ -318,25 +318,40 @@
                 kv_raw[0, :, head_columns(h)], cos_ref[...], sin_ref[...]
             )
 
-    turn_current(0, HEADS)
     pick = (lax.broadcasted_iota(jnp.int32, (16, HEAD), 1) == 0).astype(jnp.float32)
     pick = pick.astype(jnp.bfloat16)
     transposed = (((1,), (1,)), ((), ()))
-    def near_attention():
-        for h in range(HEADS):
+    def early_attention(numbers, start, stop):
+        for h in range(start, stop):
             cols = head_columns(h)
-            scores = lax.dot_general(
-                q_rot[:, cols], k_rot[:, cols], transposed, preferred_element_type=jnp.float32
-            ) * scale
-            highest = jnp.max(scores, axis=-1, keepdims=True)
-            weights = jnp.exp(scores - highest)
+            q = q_rot[:, cols]
+            scores = [
+                lax.dot_general(
+                    q, k_rot[:, cols], transposed, preferred_element_type=jnp.float32
+                ) * scale
+            ]
+            held = [kv_raw[1, :, cols]]
+            for k, number in enumerate(numbers):
+                part = pl.ds(number * LANE, LANE)
+                block = keys[part, :, cols].reshape(LANE * slots, HEAD)
+                scores.append(
+                    lax.dot_general(q, block, transposed, preferred_element_type=jnp.float32)
+                    * scale + bias_ref[16 * k : 16 * k + 1, :]
+                )
+                held.append(values[part, :, cols].reshape(LANE * slots, HEAD))
+            highest = jnp.max(scores[0], axis=-1, keepdims=True)
+            for score in scores[1:]:
+                highest = jnp.maximum(highest, jnp.max(score, axis=-1, keepdims=True))
+            weights = [jnp.exp(score - highest) for score in scores]
             top_ref[:, cols] = jnp.broadcast_to(highest, (queries, HEAD))
-            total_ref[:, cols] = fold(weights)
-            sum_ref[:, cols] = jnp.dot(
-                weights.astype(jnp.bfloat16), kv_raw[1, :, cols], preferred_element_type=jnp.float32
-            )
-
-    def gather(number):
+            total_ref[:, cols] = sum([fold(w) for w in weights[1:]], fold(weights[0]))
+            products = [
+                jnp.dot(w.astype(jnp.bfloat16), v, preferred_element_type=jnp.float32)
+                for w, v in zip(weights, held)
+            ]
+            sum_ref[:, cols] = sum(products[1:], products[0])
+
+    def gather(k, number):
         first = number * LANE
         for c in range(COLUMNS):
             for part in range(2):
@@ -347,14 +362,14 @@
             spans.append(
                 jnp.minimum(keys[first + i, :, depth:].astype(jnp.float32), seen)
             )
-        bias_ref[...] = lax.dot_general(
+        bias_ref[16 * k : 16 * (k + 1), :] = lax.dot_general(
             pick, jnp.concatenate(spans, axis=0).astype(jnp.bfloat16), transposed,
             preferred_element_type=jnp.float32,
         )
 
-    def plane(number, start, stop, last):
+    def plane(k, number, start, stop, last):
         first = number * LANE
-        bias = bias_ref[0:1, :]
+        bias = bias_ref[16 * k : 16 * k + 1, :]
         for h in range(start, stop):
             cols = head_columns(h)
             block = keys[pl.ds(first, LANE), :, cols].reshape(LANE * slots, HEAD)
@@ -390,26 +405,21 @@
 
     own_values.wait()
     half = HEADS // 2
-    number = None
     for distance in range(1, deep):
         for part in range(2):
             line(distance, part)
             side(distance - 1, part)
-            if distance == 1 and part == 0:
-                near_attention()
-                continue
-            if part == 0:
-                plane(number, half, HEADS, False)
-            else:
-                number = ordered(distance - 1)
-                gather(number)
-                plane(number, 0, half, False)
-    plane(number, half, HEADS, False)
-    for part in range(2):
-        side(deep - 1, part)
-    number = ordered(deep - 1)
-    gather(number)
-    plane(number, 0, HEADS, True)
+            if distance == 1:
+                turn_current(part * half, HEADS if part else half)
+    numbers = [ordered(k) for k in range(deep)]
+    for k in range(deep - 1):
+        gather(k, numbers[k])
+    early_attention(numbers[:-1], 0, half)
+    side(deep - 1, 0)
+    early_attention(numbers[:-1], half, HEADS)
+    side(deep - 1, 1)
+    gather(deep - 1, numbers[-1])
+    plane(deep - 1, numbers[-1], 0, HEADS, True)
 
     def sent(slot, own=False):
         for part in range(2):
@@ -467,7 +477,7 @@
             pltpu.VMEM((queries, depth), jnp.float32),
             pltpu.VMEM((queries, depth), jnp.float32),
             pltpu.VMEM((queries, depth), jnp.float32),
-            pltpu.VMEM((16, LANE * slots), jnp.float32),
+            pltpu.VMEM((16 * deep, LANE * slots), jnp.float32),
             pltpu.SemaphoreType.DMA((3,)),
             pltpu.SemaphoreType.DMA,
             pltpu.SemaphoreType.DMA((2, blocks, DIRECTIONS)),

time: 36.7 us -> 35.3 us (0.962)
  Pallas kernels: 34.1 us -> 32.7 us
    pallas_call x1, Pallas kernels: 34.1 us -> 32.7 us  [whole_rows(): pl.pallas_call(lambda *refs: span_kernel(deep, *refs), out_shape=jax.Shap...]
where the time goes in v4:
time: 35.3 us; the launch traced here: 35.1 us
  Pallas kernels  32.7 us (93%)
  local copies, waits for them, and re-layouts  1.77 us (5%)
  between operations  0.66 us (2%)
    pallas_call x1, Pallas kernels, whole_rows(): pl.pallas_call(lambda *refs: span_kernel(deep, *refs), out_shape=jax.Shap...  32.7 us
    unnamed x1, local copies, waits for them, and re-layouts  1.77 us

profile of v4, /device:TPU:0, one launch (start us, length us, event | category | flops | bytes accessed | tf_op | source)
XLA Modules:
  0.0 35.1 jit_solution(18386452467066364635)
XLA Ops:
  0.7 32.7 %shard_map.73 = bf16[128,1536]{1,0:T(8,128)(2,1)} custom-call(bf16[128,1536]{1,0:T(8,128)(2,1)} %bitcast.8, bf16[2,128,1536]{2,1,0:T(8,128)(2,1)} %bitcast.7, s32[3,2,64]{2,1,0:T(2,128)} %bitcast.10, bf16[2,32,1536]{2,1,0:T(8,128)(2,1)} %bitcast.9, s32[3,1,32]{2,1,0:T(1,128)} %bitcast.11, s32[1,1]{1,0:T(1,128)S(6)} %copy.9.refs_5_, s32[1,16]{1,0:T(1,128)} %refs_6_.1), custom_call_target="tpu_custom_call" | custom-call | tf_op jit(solution)/shard_map/pallas_call | solution.py:462
  33.4 1.8 %copy.10 = bf16[1,2,64,1536]{3,2,1,0:T(8,128)(2,1)} copy(bf16[1,2,64,1536]{3,2,1,0:T(8,128)(2,1)} %bitcast.6) | data formatting | bytes 786432

commit v5 on v1

--- a/solution.py
+++ b/solution.py
@@ -186,8 +186,8 @@
 
 
 def span_kernel(
-    deep, q_hbm, kv_hbm, cur_pos_ref, cache_ref, cache_pos_ref, count_ref, visible_ref, out_ref,
-    q_raw, kv_raw, q_rot, k_rot, cos_ref, sin_ref, keys, values, bias_ref, load_sem, own_sem,
+    deep, q_hbm, kv_hbm, cur_pos_ref, cache_ref, cache_pos_hbm, count_ref, visible_ref, out_ref,
+    q_raw, kv_raw, q_rot, k_rot, cos_ref, sin_ref, keys, values, bias_ref, kept_pos, load_sem, own_sem,
     send_sem, recv_sem,
 ):
     me = lax.axis_index("tm")
@@ -207,6 +207,8 @@
             barrier, inc=1, device_id={"tm": device}, device_id_type=pl.DeviceIdType.MESH
         )
 
+    load_pos = pltpu.make_async_copy(cache_pos_hbm, kept_pos, load_sem.at[2])
+    load_pos.start()
     greet(core_other)
     greet(column_other)
     pl.when(place > 0)(lambda: greet(me - LANE))
@@ -219,7 +221,8 @@
     load_kv.start()
     own_values.start()
 
-    cosine, sine = turn_tables(cache_pos_ref[0:1, :], cache_pos_ref[1:2, :], cache_pos_ref[2:3, :])
+    load_pos.wait()
+    cosine, sine = turn_tables(kept_pos[0], kept_pos[1], kept_pos[2])
     for h in range(HEADS):
         keys[me, :, head_columns(h)] = turn(cache_ref[0, :, head_columns(h)], cosine, sine)
     row = lax.broadcasted_iota(jnp.int32, (slots, HEAD), 0)
@@ -291,6 +294,10 @@
             pl.when(place >= distance)(lambda: relay(column_other - distance * LANE))
             pl.when(place < deep - distance)(lambda: relay(column_other + distance * LANE))
 
+    for distance in range(1, deep):
+        for part in range(2):
+            line(distance, part)
+            side(distance - 1, part)
     load_q.wait()
     load_kv.wait()
     queries = q_raw.shape[0]
@@ -311,11 +318,6 @@
             )
 
     turn_current(0, HEADS)
-    for distance in range(1, deep):
-        for part in range(2):
-            line(distance, part)
-        for part in range(2):
-            side(distance - 1, part)
     for part in range(2):
         side(deep - 1, part)
     for far in range(deep):
@@ -399,7 +401,7 @@
     output = pl.pallas_call(
         lambda *refs: span_kernel(deep, *refs),
         out_shape=jax.ShapeDtypeStruct((queries, depth), jnp.bfloat16),
-        in_specs=[hbm, hbm, vmem, vmem, vmem, smem, smem],
+        in_specs=[hbm, hbm, vmem, vmem, hbm, smem, smem],
         out_specs=vmem,
         scratch_shapes=[
             pltpu.VMEM((queries, depth), jnp.bfloat16),
@@ -411,7 +413,8 @@
             pltpu.VMEM((blocks, slots, depth + HEAD), jnp.bfloat16),
             pltpu.VMEM((blocks, slots, depth), jnp.bfloat16),
             pltpu.VMEM((blocks * slots, HEAD), jnp.bfloat16),
-            pltpu.SemaphoreType.DMA((2,)),
+            pltpu.VMEM((3, 1, slots), jnp.int32),
+            pltpu.SemaphoreType.DMA((3,)),
             pltpu.SemaphoreType.DMA,
             pltpu.SemaphoreType.DMA((2, blocks, DIRECTIONS)),
             pltpu.SemaphoreType.DMA((2, blocks)),
@@ -422,7 +425,7 @@
         cur_kv.reshape(2, queries, depth),
         cur_pos.reshape(3, tile_rows, columns),
         cache_kv.reshape(2, slots, depth),
-        cache_pos.reshape(3, slots),
+        jnp.transpose(cache_pos, (1, 0, 2)),
         counts,
         visible,
     )

time: 35.1 us -> 33.9 us (0.966)
  local copies, waits for them, and re-layouts: 3.02 us -> 1.77 us
    unnamed x4 -> x1, local copies, waits for them, and re-layouts: 3.02 us -> 1.77 us
where the time goes in v5:
time: 33.9 us; the launch traced here: 33.7 us
  Pallas kernels  31.3 us (92%)
  local copies, waits for them, and re-layouts  1.77 us (5%)
  between operations  0.66 us (2%)
    pallas_call x1, Pallas kernels, whole_rows(): pl.pallas_call(lambda *refs: span_kernel(deep, *refs), out_shape=jax.Shap...  31.3 us
    unnamed x1, local copies, waits for them, and re-layouts  1.77 us

profile of v5, /device:TPU:1, one launch (start us, length us, event | category | flops | bytes accessed | tf_op | source)
XLA Modules:
  0.0 33.7 jit_solution(7441061534678494690)
XLA Ops:
  0.7 31.3 %shard_map.73 = bf16[128,1536]{1,0:T(8,128)(2,1)} custom-call(bf16[128,1536]{1,0:T(8,128)(2,1)} %bitcast.8, bf16[2,128,1536]{2,1,0:T(8,128)(2,1)} %bitcast.7, s32[3,2,64]{2,1,0:T(2,128)} %bitcast.10, bf16[2,32,1536]{2,1,0:T(8,128)(2,1)} %bitcast.9, s32[3,1,32]{2,1,0:T(1,128)} %bitcast.11, s32[1,1]{1,0:T(1,128)S(6)} %copy.9.refs_5_, s32[1,16]{1,0:T(1,128)} %refs_6_.1), custom_call_target="tpu_custom_call" | custom-call | tf_op jit(solution)/shard_map/pallas_call | solution.py:401
  31.9 1.8 %copy.10 = bf16[1,2,64,1536]{3,2,1,0:T(8,128)(2,1)} copy(bf16[1,2,64,1536]{3,2,1,0:T(8,128)(2,1)} %bitcast.6) | data formatting | bytes 786432
